TPU v7x, 32 devices: a whole 2x2x4 slice. The times are simulated.
32 devices in a mesh: clips: 2 (over y), tok: 4 (over z), head: 4 (over x, core).
Axes of the slice: x: 2, y: 2, z: 4, core: 2. Of those that a mesh axis runs over, the one named last changes fastest.
Arguments:
- query: bfloat16 [24, 256, 1536], P(('clips', 'tok'), 'head'), parts along dimension 0, may hold values from -16 to 16, as said below
- key: bfloat16 [24, 256, 1536], P(('clips', 'tok'), 'head'), parts along dimension 0, may hold values from -16 to 16
- value: bfloat16 [24, 256, 1536], P(('clips', 'tok'), 'head'), parts along dimension 0, may hold values from -6 to 6
- valid_rows: int32 [24], P(('clips', 'tok')), parts along dimension 0, may hold values from 1 to 8, as said below
Outputs:
- attended: bfloat16 [24, 256, 1536], P(('clips', 'tok'), 'head'), parts along dimension 0
There are 2 independent parts, one for each index of `clips`. A program takes and returns all parts, laid end to end along the dimension named above; each array names one. Nothing has to cross between parts.
Inputs may be any that keep to these rules, and one draw needn't show every extreme that they name: Entries of query and key lie within -16 and 16. `valid_rows`: tiles outside the last height-tile row have all 8 rows real; tiles of the last height-tile row each have their own count.
All inputs are finite; a program needn't handle non-finite values.
Results may differ from a plain program's by a relative error of at most 0.0031.
Values may be sent and summed in bfloat16 or wider, within the bound.
A program may use at most 64 MiB of HBM per device.

v0:
```python
import math

import jax
import jax.numpy as jnp
from jax import lax
from jax.sharding import PartitionSpec as P

HEAD_DIM = 128
TILE_H = 8
TILE_W = 8
TIME_TILES = 4


def shifted(block, axis, distance):
    devices = range(lax.axis_size(axis))
    route = [(i - distance, i) for i in devices if i - distance in devices]
    return lax.ppermute(block, axis, route)


def blank_piece(piece):
    return tuple((jnp.zeros_like(member) for member in piece))


def clear_counts(piece, keep):
    return (piece[0], piece[1], jnp.where(keep, piece[2], 0))


def body(query, key, value, valid_rows):
    q_heads, k_heads, v_heads = (
        lax.all_to_all(query, "head", split_axis=2, concat_axis=1, tiled=True),
        lax.all_to_all(key, "head", split_axis=2, concat_axis=1, tiled=True),
        lax.all_to_all(value, "head", split_axis=2, concat_axis=1, tiled=True),
    )
    width = q_heads.shape[0]
    tile_len = q_heads.shape[1]
    local = q_heads.shape[2] // HEAD_DIM
    scale = 1.0 / math.sqrt(HEAD_DIM)
    rows_grid = lax.axis_size("tok") // TIME_TILES
    height = lax.axis_index("tok") % rows_grid
    own = (k_heads, v_heads, valid_rows)
    pieces = []
    for down in (-1, 0, 1):
        for side in (-1, 0, 1):
            if down == 0 and side == 0:
                pieces.append(own)
            elif side != 0 and rows_grid == 1:
                pieces.append(blank_piece(own))
            else:
                moved = shifted((own[0], own[1], own[2]), "tok", -(down * rows_grid + side))
                if side != 0:
                    moved = clear_counts(moved, (height + side >= 0) & (height + side < rows_grid))
                pieces.append(moved)
    padded = [
        (
            jnp.pad(piece[0], ((1, 1), (0, 0), (0, 0))),
            jnp.pad(piece[1], ((1, 1), (0, 0), (0, 0))),
            jnp.pad(piece[2], (1, 1)),
        )
        for piece in pieces
    ]
    counts_all = jnp.stack([piece[2] for piece in padded])
    row_index = jnp.arange(tile_len) // TILE_W % TILE_H

    def attend(number):
        tile = number // local
        start = number % local * HEAD_DIM
        block_keys = jnp.concatenate(
            [
                lax.dynamic_slice(piece[0], (tile, 0, start), (3, tile_len, HEAD_DIM))
                for piece in padded
            ],
            0,
        ).reshape(-1, HEAD_DIM)
        block_values = jnp.concatenate(
            [
                lax.dynamic_slice(piece[1], (tile, 0, start), (3, tile_len, HEAD_DIM))
                for piece in padded
            ],
            0,
        ).reshape(-1, HEAD_DIM)
        counts = lax.dynamic_slice_in_dim(counts_all, tile, 3, 1)
        mask = (row_index[None, None, :] < counts[:, :, None]).reshape(-1)
        queries = lax.dynamic_slice(q_heads, (tile, 0, start), (1, tile_len, HEAD_DIM))[0]
        scores = (
            jnp.einsum("qd,kd->qk", queries, block_keys, preferred_element_type=jnp.float32) * scale
        )
        scores = jnp.where(mask[None, :], scores, -jnp.inf)
        largest = jnp.max(scores, axis=-1, keepdims=True)
        weight = jnp.exp(scores - largest)
        total = jnp.sum(weight, axis=-1, keepdims=True)
        rounded = weight.astype(jnp.bfloat16)
        summed = jnp.dot(rounded, block_values, preferred_element_type=jnp.float32)
        return (summed / total).astype(jnp.bfloat16)

    results = lax.map(attend, jnp.arange(width * local, dtype=jnp.int32))
    attended = results.reshape(width, local, tile_len, HEAD_DIM).transpose(0, 2, 1, 3)
    attended = attended.reshape(width, tile_len, local * HEAD_DIM)
    return lax.all_to_all(attended, "head", split_axis=1, concat_axis=2, tiled=True)


def solution(mesh):
    placed = (
        P(("clips", "tok"), "head", None),
        P(("clips", "tok"), "head", None),
        P(("clips", "tok"), "head", None),
        P(("clips", "tok")),
    )
    return jax.shard_map(
        body,
        mesh=mesh,
        in_specs=placed,
        out_specs=P(("clips", "tok"), "head", None),
        check_vma=False,
    )
```

profile of v0, /device:TPU:0, one launch (start us, length us, event | category | flops | bytes accessed | tf_op | source)
XLA Modules:
  0.0 204.0 jit_solution(15187029604609117367)
XLA Ops:
  0.0 2.5 %copy.28 = bf16[3,64,1536]{1,0,2:T(4,128)(2,1)S(1)} copy(bf16[3,64,1536]{2,1,0:T(8,128)(2,1)} %param.7) | data formatting | bytes 1179648 | tf_op args[1]
  2.5 2.2 %reshape.59 = bf16[4,2,36864]{2,1,0:T(2,128)(2,1)} reshape(bf16[1536,3,64]{2,1,0:T(4,128)(2,1)S(1)} %bitcast.73) | data formatting | bytes 1179648
  4.7 4.2 %all-to-all-start.1 = ((bf16[4,2,36864]{2,1,0:T(2,128)(2,1)}), bf16[4,2,36864]{2,1,0:T(2,128)(2,1)S(1)}, u32[]{:S(2)}, u32[]{:S(2)}) async-start(bf16[4,2,36864]{2,1,0:T(2,128)(2,1)} %reshape.59), calls=%async_computation.1 | async-start | bytes 1179648 | tf_op jit(solution)/shard_map/all_to_all | solution.py:31
  10.0 2.2 %reshape.61 = bf16[4,2,36864]{2,1,0:T(2,128)(2,1)} reshape(bf16[1536,3,64]{2,1,0:T(4,128)(2,1)S(1)} %bitcast.74) | data formatting | bytes 1179648
  12.1 6.3 %all-to-all-done.1 = bf16[4,2,36864]{2,1,0:T(2,128)(2,1)S(1)} async-done(((bf16[4,2,36864]{2,1,0:T(2,128)(2,1)}), bf16[4,2,36864]{2,1,0:T(2,128)(2,1)S(1)}, u32[]{:S(2)}, u32[]{:S(2)}) %all-to-all-start.1) | async-done | bytes 589856 | tf_op jit(solution)/shard_map/all_to_all | solution.py:31
  18.4 3.5 %all-to-all-start.2 = ((bf16[4,2,36864]{2,1,0:T(2,128)(2,1)}), bf16[4,2,36864]{2,1,0:T(2,128)(2,1)S(1)}, u32[]{:S(2)}, u32[]{:S(2)}) async-start(bf16[4,2,36864]{2,1,0:T(2,128)(2,1)} %reshape.61), calls=%async_computation.2 | async-start | bytes 1179648 | tf_op jit(solution)/shard_map/all_to_all | solution.py:32
  23.0 2.0 copy.29
  25.0 1.4 collective-permute-start.3
  26.4 5.6 %collective-permute-start.2 = (bf16[3,256,384]{2,1,0:T(8,128)(2,1)}, bf16[3,256,384]{2,1,0:T(8,128)(2,1)}, u32[]{:S(2)}, u32[]{:S(2)}) collective-permute-start(bf16[3,256,384]{2,1,0:T(8,128)(2,1)} %bitcast.9), channel_id=1, source_target_pairs={{0,4},{4,8},{8,12},{1,5},{5,9},{9,13},{2,6},{6,10},{10,14},{3,7},{... | collective-permute-start | bytes 1769480 | tf_op jit(solution)/shard_map/ppermute | solution.py:17
  33.0 2.0 copy.31
  35.0 1.3 collective-permute-start.5
  36.3 5.4 %collective-permute-start.4 = (bf16[3,256,384]{2,1,0:T(8,128)(2,1)}, bf16[3,256,384]{2,1,0:T(8,128)(2,1)}, u32[]{:S(2)}, u32[]{:S(2)}) collective-permute-start(bf16[3,256,384]{2,1,0:T(8,128)(2,1)} %bitcast.12), channel_id=1, source_target_pairs={{0,4},{4,8},{8,12},{1,5},{5,9},{9,13},{2,6},{6,10},{10,14},{3,7},{... | collective-permute-start | bytes 1769480 | tf_op jit(solution)/shard_map/ppermute | solution.py:17
  42.8 2.2 %reshape.57 = bf16[4,2,36864]{2,1,0:T(2,128)(2,1)} reshape(bf16[1536,3,64]{2,1,0:T(4,128)(2,1)S(1)} %bitcast.75) | data formatting | bytes 1179648
  44.9 4.2 %all-to-all-start = ((bf16[4,2,36864]{2,1,0:T(2,128)(2,1)}), bf16[4,2,36864]{2,1,0:T(2,128)(2,1)}, u32[]{:S(2)}, u32[]{:S(2)}) async-start(bf16[4,2,36864]{2,1,0:T(2,128)(2,1)} %reshape.57), calls=%async_computation | async-start | bytes 1179648 | tf_op jit(solution)/shard_map/all_to_all | solution.py:30
  49.1 2.8 %collective-permute-start = (s32[3]{0:T(128)S(1)}, s32[3]{0:T(128)S(1)}, u32[]{:S(2)}, u32[]{:S(2)}) collective-permute-start(s32[3]{0:T(128)S(1)} %copy-done.2), channel_id=1, source_target_pairs={{0,4},{4,8},{8,12},{1,5},{5,9},{9,13},{2,6},{6,10},{10,14},{3,7},{... | collective-permute-start | bytes 44 | tf_op jit(solution)/shard_map/ppermute | solution.py:17
  52.0 5.3 %collective-permute-done = s32[3]{0:T(128)S(1)} collective-permute-done((s32[3]{0:T(128)S(1)}, s32[3]{0:T(128)S(1)}, u32[]{:S(2)}, u32[]{:S(2)}) %collective-permute-start) | collective-permute-done | bytes 44 | tf_op jit(solution)/shard_map/ppermute | solution.py:17
  57.3 1.3 collective-permute-start.1
  58.7 4.6 %collective-permute-done.1 = s32[3]{0:T(128)S(1)} collective-permute-done((s32[3]{0:T(128)S(1)}, s32[3]{0:T(128)S(1)}, u32[]{:S(2)}, u32[]{:S(2)}) %collective-permute-start.1) | collective-permute-done | bytes 44 | tf_op jit(solution)/shard_map/ppermute | solution.py:17
  63.5 1.2 pad.60
  64.6 1.2 pad.63
  65.8 2.7 %reshape.58 = bf16[1536,3,64]{2,1,0:T(4,128)(2,1)S(1)} reshape(bf16[4,2,36864]{2,1,0:T(2,128)(2,1)} %all-to-all-done) | data formatting | bytes 1179648
  68.5 1.9 copy.27
  70.4 2.1 %pad.61 = bf16[5,256,384]{2,1,0:T(8,128)(2,1)} pad(bf16[3,256,384]{2,1,0:T(8,128)(2,1)} %collective-permute-done.3, bf16[]{:T(256)} %constant.114.clone.1), padding=1_1x0_0x0_0 | pad | bytes 1572866 | tf_op jit(solution)/shard_map/jit(_pad)/pad | solution.py:55
  72.5 2.2 %pad.59 = bf16[5,256,384]{2,1,0:T(8,128)(2,1)} pad(bf16[3,256,384]{2,1,0:T(8,128)(2,1)} %collective-permute-done.2, bf16[]{:T(256)} %constant.114.clone.1), padding=1_1x0_0x0_0 | pad | bytes 1572866 | tf_op jit(solution)/shard_map/jit(_pad)/pad | solution.py:55
  74.7 2.1 %pad.64 = bf16[5,256,384]{2,1,0:T(8,128)(2,1)} pad(bf16[3,256,384]{2,1,0:T(8,128)(2,1)} %collective-permute-done.5, bf16[]{:T(256)} %constant.114.clone.1), padding=1_1x0_0x0_0 | pad | bytes 1572866 | tf_op jit(solution)/shard_map/jit(_pad)/pad | solution.py:56
  76.8 2.1 %pad.62 = bf16[5,256,384]{2,1,0:T(8,128)(2,1)} pad(bf16[3,256,384]{2,1,0:T(8,128)(2,1)} %collective-permute-done.4, bf16[]{:T(256)} %constant.114.clone.1), padding=1_1x0_0x0_0 | pad | bytes 1572866 | tf_op jit(solution)/shard_map/jit(_pad)/pad | solution.py:56
  79.1 108.1 %while.14 = (s32[]{:T(128)}, bf16[9,256,128]{1,2,0:T(8,128)(2,1)}, s32[9]{0:T(128)S(1)}, s32[9,5]{0,1:T(8,128)S(1)}, bf16[3,256,384]{2,1,0:T(8,128)(2,1)}, /*ind...) while((s32[]{:T(128)}, bf16[9,256,128]{1,2,0:T(8,128)(2,1)}, ...), condition=%wide.region_3.4_spmd.clone, body=%wide.region_0.3_spmd.clone.sunk | while | flops 918432768 | bytes 35228752 | solution.py:95
  85.9 2.0 fusion.33
  87.9 1.1 fusion.34
  89.0 1.3 fusion.35
  97.9 2.0 fusion.33
  101.0 1.3 fusion.35
  109.9 2.0 fusion.33
  113.1 1.3 fusion.35
  121.9 2.0 fusion.33
  125.1 1.3 fusion.35
  133.9 2.0 fusion.33
  137.1 1.3 fusion.35
  145.9 2.0 fusion.33
  149.1 1.3 fusion.35
  157.9 2.0 fusion.33
  161.1 1.3 fusion.35
  169.9 2.0 fusion.33
  173.1 1.3 fusion.35
  181.9 2.0 fusion.33
  185.1 1.3 fusion.35
  187.2 1.5 copy.34
  188.7 14.3 %all_to_all.72 = bf16[3,256,384]{2,0,1:T(4,128)(2,1)S(1)} all-to-all(bf16[3,256,384]{2,0,1:T(4,128)(2,1)S(1)} %copy.34), channel_id=1, replica_groups=mesh['clips'=2,'tok'=4,'head'=4] {'head'}, dimensions={1} | all-to-all | bytes 1179648 | tf_op jit(solution)/shard_map/all_to_all | solution.py:98
  (253 shorter events, 63.8 us)
Async XLA Ops:
  2.5 6.4 %copy-start = (bf16[3,64,1536]{2,1,0:T(8,128)(2,1)S(1)}, bf16[3,64,1536]{2,1,0:T(8,128)(2,1)}, u32[]{:S(2)}) copy-start(bf16[3,64,1536]{2,1,0:T(8,128)(2,1)} %param.8) | copy-start | bytes 1769476
  4.7 13.8 %all-to-all-start.1 = ((bf16[4,2,36864]{2,1,0:T(2,128)(2,1)}), bf16[4,2,36864]{2,1,0:T(2,128)(2,1)S(1)}, u32[]{:S(2)}, u32[]{:S(2)}) async-start(bf16[4,2,36864]{2,1,0:T(2,128)(2,1)} %reshape.59), calls=%async_computation.1 | async-start | bytes 1179648 | tf_op jit(solution)/shard_map/all_to_all | solution.py:31
  18.4 13.6 %all-to-all-start.2 = ((bf16[4,2,36864]{2,1,0:T(2,128)(2,1)}), bf16[4,2,36864]{2,1,0:T(2,128)(2,1)S(1)}, u32[]{:S(2)}, u32[]{:S(2)}) async-start(bf16[4,2,36864]{2,1,0:T(2,128)(2,1)} %reshape.61), calls=%async_computation.2 | async-start | bytes 1179648 | tf_op jit(solution)/shard_map/all_to_all | solution.py:32
  25.0 16.7 %copy-start.1 = (bf16[3,64,1536]{2,1,0:T(8,128)(2,1)S(1)}, bf16[3,64,1536]{2,1,0:T(8,128)(2,1)}, u32[]{:S(2)}) copy-start(bf16[3,64,1536]{2,1,0:T(8,128)(2,1)} %param.6) | copy-start | bytes 1769476
  25.0 45.4 %collective-permute-start.3 = (bf16[3,256,384]{2,1,0:T(8,128)(2,1)}, bf16[3,256,384]{2,1,0:T(8,128)(2,1)}, u32[]{:S(2)}, u32[]{:S(2)}) collective-permute-start(bf16[3,256,384]{2,1,0:T(8,128)(2,1)} %bitcast.9), channel_id=1, source_target_pairs={{4,0},{8,4},{12,8},{5,1},{9,5},{13,9},{6,2},{10,6},{14,10},{7,3},{... | collective-permute-start | bytes 1769480 | tf_op jit(solution)/shard_map/ppermute | solution.py:17
  26.4 46.1 %collective-permute-start.2 = (bf16[3,256,384]{2,1,0:T(8,128)(2,1)}, bf16[3,256,384]{2,1,0:T(8,128)(2,1)}, u32[]{:S(2)}, u32[]{:S(2)}) collective-permute-start(bf16[3,256,384]{2,1,0:T(8,128)(2,1)} %bitcast.9), channel_id=1, source_target_pairs={{0,4},{4,8},{8,12},{1,5},{5,9},{9,13},{2,6},{6,10},{10,14},{3,7},{... | collective-permute-start | bytes 1769480 | tf_op jit(solution)/shard_map/ppermute | solution.py:17
  35.0 39.6 %collective-permute-start.5 = (bf16[3,256,384]{2,1,0:T(8,128)(2,1)}, bf16[3,256,384]{2,1,0:T(8,128)(2,1)}, u32[]{:S(2)}, u32[]{:S(2)}) collective-permute-start(bf16[3,256,384]{2,1,0:T(8,128)(2,1)} %bitcast.12), channel_id=1, source_target_pairs={{4,0},{8,4},{12,8},{5,1},{9,5},{13,9},{6,2},{10,6},{14,10},{7,3},{... | collective-permute-start | bytes 1769480 | tf_op jit(solution)/shard_map/ppermute | solution.py:17
  36.3 40.5 %collective-permute-start.4 = (bf16[3,256,384]{2,1,0:T(8,128)(2,1)}, bf16[3,256,384]{2,1,0:T(8,128)(2,1)}, u32[]{:S(2)}, u32[]{:S(2)}) collective-permute-start(bf16[3,256,384]{2,1,0:T(8,128)(2,1)} %bitcast.12), channel_id=1, source_target_pairs={{0,4},{4,8},{8,12},{1,5},{5,9},{9,13},{2,6},{6,10},{10,14},{3,7},{... | collective-permute-start | bytes 1769480 | tf_op jit(solution)/shard_map/ppermute | solution.py:17
  42.7 6.3 %copy-start.2 = (s32[3]{0:T(128)S(1)}, s32[3]{0:T(128)}, u32[]{:S(2)}) copy-start(s32[3]{0:T(128)} %param.9) | copy-start | bytes 40
  44.9 20.9 %all-to-all-start = ((bf16[4,2,36864]{2,1,0:T(2,128)(2,1)}), bf16[4,2,36864]{2,1,0:T(2,128)(2,1)}, u32[]{:S(2)}, u32[]{:S(2)}) async-start(bf16[4,2,36864]{2,1,0:T(2,128)(2,1)} %reshape.57), calls=%async_computation | async-start | bytes 1179648 | tf_op jit(solution)/shard_map/all_to_all | solution.py:30
  49.1 8.2 %collective-permute-start = (s32[3]{0:T(128)S(1)}, s32[3]{0:T(128)S(1)}, u32[]{:S(2)}, u32[]{:S(2)}) collective-permute-start(s32[3]{0:T(128)S(1)} %copy-done.2), channel_id=1, source_target_pairs={{0,4},{4,8},{8,12},{1,5},{5,9},{9,13},{2,6},{6,10},{10,14},{3,7},{... | collective-permute-start | bytes 44 | tf_op jit(solution)/shard_map/ppermute | solution.py:17
  57.3 5.9 %collective-permute-start.1 = (s32[3]{0:T(128)S(1)}, s32[3]{0:T(128)S(1)}, u32[]{:S(2)}, u32[]{:S(2)}) collective-permute-start(s32[3]{0:T(128)S(1)} %copy-done.2), channel_id=1, source_target_pairs={{4,0},{8,4},{12,8},{5,1},{9,5},{13,9},{6,2},{10,6},{14,10},{7,3},{... | collective-permute-start | bytes 44 | tf_op jit(solution)/shard_map/ppermute | solution.py:17
where the time goes:
time: 206 us; the launch traced here: 204 us
  local copies, waits for them, and re-layouts  83.7 us (41%)
  matrix products  30.1 us (15%)
  starting transfers between devices  29.6 us (14%)
  loops' own time  18.8 us (9%)
  waiting for transfers between devices  16.2 us (8%)
  blocking collectives  14.3 us (7%)
  other arithmetic  11.1 us (5%)
    while x126, local copies, waits for them, and re-layouts  33.3 us
    another operation x1, loops' own time, body(): results = lax.map(attend, jnp.arange(width * local, dtype=jnp.int32))  18.8 us
    dot_general x9, matrix products, attend(): jnp.einsum('qd,kd->qk', queries, block_keys, preferred_element_type=jnp.f...  18.3 us
    ppermute x6, starting transfers between devices, shifted(): return lax.ppermute(block, axis, route)  17.8 us
    unnamed x16, local copies, waits for them, and re-layouts  15.9 us
    all_to_all x1, blocking collectives, body(): lax.all_to_all(attended, 'head', split_axis=1, concat_axis=2, tiled=True)  14.3 us
    dot_general x9, matrix products, attend(): summed = jnp.dot(rounded, block_values, preferred_element_type=jnp.float32)  11.8 us
    reduce_sum x9, other arithmetic, attend(): total = jnp.sum(weight, axis=-1, keepdims=True)  10.3 us
  transfers between devices with their start and end apart: 9, of which 3 were waited for; matrix products, arithmetic and copies ran while one was open for 13% of the time, Pallas kernels for 0%

commit v1 on v0

v1 whole, which is shorter than its diff:
```python
import functools
import math

import jax
import jax.numpy as jnp
from jax import lax
from jax.experimental import pallas as pl
from jax.experimental.pallas import tpu as pltpu
from jax.sharding import PartitionSpec as P

HEAD_DIM = 128
TILE_H = 8
TILE_W = 8
TIME_TILES = 4
MESH = pl.DeviceIdType.MESH
GAIN = math.log2(math.e) / math.sqrt(HEAD_DIM)


def window_slots(rows_grid):
    sides = (-1, 0, 1) if rows_grid > 1 else (0,)
    around = [(down, side) for down in (-1, 0, 1) for side in sides if (down, side) != (0, 0)]
    return [(0, 0)] + around


def kernel(
    heads_axis, rows_grid,
    q_hbm, k_hbm, v_hbm, bias_hbm, out_hbm,
    q_buf, k_buf, v_buf, bias_buf, s_buf, p_buf, inv_buf, o_buf,
    local_sem, qx_send, qx_recv, kx_send, kx_recv, vx_send, vx_recv,
    bz_send, bz_recv, kz_send, kz_recv, vz_send, vz_recv, ox_send, ox_recv,
):
    slots = window_slots(rows_grid)
    width, part = q_hbm.shape[0], q_hbm.shape[1]
    tile_len, feats = q_buf.shape[1], q_buf.shape[2]
    local = feats // HEAD_DIM
    me = lax.axis_index("head")
    tok = lax.axis_index("tok")
    time, height = tok // rows_grid, tok % rows_grid
    steps = range(1, heads_axis)
    far_first = list(reversed(steps))

    def exists(j):
        down, side = slots[j]
        ok = (time + down >= 0) & (time + down < TIME_TILES)
        if side != 0:
            ok = ok & (height + side >= 0) & (height + side < rows_grid)
        return ok

    def around(j):
        return tok + slots[j][0] * rows_grid + slots[j][1]

    def opposite(j):
        return slots.index((-slots[j][0], -slots[j][1]))

    def peer(s):
        return me ^ s

    def rows(g):
        return pl.ds(pl.multiple_of(g * part, part), part)

    def cols(g):
        return pl.ds(pl.multiple_of(g * feats, feats), feats)

    def head_cols(h):
        return pl.ds(pl.multiple_of(h * HEAD_DIM, HEAD_DIM), HEAD_DIM)

    def global_cols(g, h):
        return pl.ds(pl.multiple_of((g * local + h) * HEAD_DIM, HEAD_DIM), HEAD_DIM)

    def remote(src, dst, send, recv, device):
        return pltpu.make_async_remote_copy(
            src_ref=src, dst_ref=dst, send_sem=send, recv_sem=recv,
            device_id=device, device_id_type=MESH,
        )

    def qx(s, owner):
        return remote(q_hbm.at[:, :, cols(peer(s))], q_buf.at[:, rows(owner), :],
                      qx_send.at[s], qx_recv.at[s], {"head": peer(s)})

    def kx(s, owner):
        return remote(k_hbm.at[:, :, cols(peer(s))], k_buf.at[0, :, rows(owner), :],
                      kx_send.at[s], kx_recv.at[s], {"head": peer(s)})

    def vx(h, s, owner):
        return remote(v_hbm.at[:, :, global_cols(peer(s), h)],
                      v_buf.at[0, :, rows(owner), head_cols(h)],
                      vx_send.at[h, s], vx_recv.at[h, s], {"head": peer(s)})

    def kz(j, s, slot):
        src = k_hbm.at[:, :, cols(me)] if s == 0 else k_buf.at[0, :, rows(peer(s)), :]
        return remote(src, k_buf.at[slot, :, rows(peer(s)), :],
                      kz_send.at[j, s], kz_recv.at[slot, s], {"tok": around(j)})

    def vz(j, h, s, slot):
        src = v_hbm.at[:, :, global_cols(me, h)] if s == 0 else v_buf.at[0, :, rows(peer(s)), head_cols(h)]
        return remote(src, v_buf.at[slot, :, rows(peer(s)), head_cols(h)],
                      vz_send.at[j, h, s], vz_recv.at[slot, h, s], {"tok": around(j)})

    def bz(j, slot):
        return remote(bias_hbm, bias_buf.at[slot], bz_send.at[j], bz_recv.at[slot], {"tok": around(j)})

    def ox(h, s, owner):
        return remote(o_buf.at[:, rows(peer(s)), head_cols(h)],
                      out_hbm.at[:, :, global_cols(owner, h)],
                      ox_send.at[h, s], ox_recv.at[h, s], {"head": peer(s)})

    def each_neighbour(act):
        for j in range(1, len(slots)):
            pl.when(exists(j))(functools.partial(act, j))

    local_q = pltpu.make_async_copy(q_hbm.at[:, :, cols(me)], q_buf.at[:, rows(me), :], local_sem.at[0])
    local_k = pltpu.make_async_copy(k_hbm.at[:, :, cols(me)], k_buf.at[0, :, rows(me), :], local_sem.at[1])
    local_v = pltpu.make_async_copy(v_hbm.at[:, :, cols(me)], v_buf.at[0, :, rows(me), :], local_sem.at[2])
    local_b = pltpu.make_async_copy(bias_hbm, bias_buf.at[0], local_sem.at[3])

    barrier = pltpu.get_barrier_semaphore()
    for s in steps:
        pl.semaphore_signal(barrier, inc=1, device_id={"head": peer(s)}, device_id_type=MESH)
    partners = heads_axis - 1

    def greet(j):
        pl.semaphore_signal(barrier, inc=1, device_id={"tok": around(j)}, device_id_type=MESH)

    each_neighbour(greet)
    for j in range(1, len(slots)):
        partners = partners + jnp.where(exists(j), 1, 0)
    for copy in (local_q, local_k, local_v, local_b):
        copy.start()
    pl.semaphore_wait(barrier, partners)

    each_neighbour(lambda j: bz(j, opposite(j)).start())
    for s in far_first:
        kx(s, me).start()
    each_neighbour(lambda j: kz(j, 0, opposite(j)).start())
    for s in far_first:
        qx(s, me).start()
    for h in range(local):
        for s in far_first:
            vx(h, s, me).start()

    for j in range(1, len(slots)):
        @pl.when(jnp.logical_not(exists(j)))
        def _(j=j):
            k_buf[j] = jnp.zeros(k_buf.shape[1:], k_buf.dtype)
            v_buf[j] = jnp.zeros(v_buf.shape[1:], v_buf.dtype)
            bias_buf[j] = jnp.full(bias_buf.shape[1:], -jnp.inf, bias_buf.dtype)

    order = [1] + [s for s in far_first if s != 1] if heads_axis > 1 else []
    for s in order:
        kx(s, peer(s)).wait_recv()
        each_neighbour(lambda j, s=s: kz(j, s, opposite(j)).start())
    near = [s for s in steps if s == 1]
    later = [s for s in order if s != 1]
    for h in range(local):
        each_neighbour(lambda j, h=h: vz(j, h, 0, opposite(j)).start())
        for s in near:
            vx(h, s, peer(s)).wait_recv()
            each_neighbour(lambda j, h=h, s=s: vz(j, h, s, opposite(j)).start())

    for copy in (local_q, local_k, local_v, local_b):
        copy.wait()
    for s in steps:
        qx(s, peer(s)).wait_recv()

    def keys_in(j):
        bz(j, j).wait_recv()
        for s in range(heads_axis):
            kz(j, s, j).wait_recv()

    each_neighbour(keys_in)

    def window(c):
        return [(j, n) for j in range(len(slots)) for n in range(width) if abs(n - c) <= 1]

    def weigh(h, carry):
        for c in range(width):
            scratch = s_buf.at[c % s_buf.shape[0]]
            q = q_buf[c, :, head_cols(h)]
            top = None
            for i, (j, n) in enumerate(window(c)):
                s = lax.dot_general(q, k_buf[j, n, :, head_cols(h)], (((1,), (1,)), ((), ())),
                                    preferred_element_type=jnp.float32)
                s = s + bias_buf[j, n, 0:1, :]
                scratch[:, i * tile_len:(i + 1) * tile_len] = s
                for half in range(0, tile_len, 128):
                    piece = s[:, half:half + 128]
                    top = piece if top is None else jnp.maximum(top, piece)
            largest = jnp.max(top, axis=-1, keepdims=True)
            total = None
            for i in range(len(window(c))):
                for half in range(0, tile_len, 128):
                    at = slice(i * tile_len + half, i * tile_len + half + 128)
                    weight = jnp.exp2((scratch[:, at] - largest) * GAIN)
                    total = weight if total is None else total + weight
                    p_buf[h, c, :, at] = weight.astype(jnp.bfloat16)
            inverse = 1.0 / jnp.sum(total, axis=-1, keepdims=True)
            inv_buf[h, c] = jnp.broadcast_to(inverse, (tile_len, HEAD_DIM))
        for s in later:
            vx(h, s, peer(s)).wait_recv()
            each_neighbour(lambda j, s=s: vz(j, h, s, opposite(j)).start())
        return carry

    lax.fori_loop(0, local, weigh, 0)

    def local_out(h):
        return pltpu.make_async_copy(o_buf.at[:, rows(me), head_cols(h)],
                                     out_hbm.at[:, :, global_cols(me, h)], local_sem.at[4 + h])

    def mix(h, carry):
        def values_in(j):
            for s in range(heads_axis):
                vz(j, h, s, j).wait_recv()

        each_neighbour(values_in)
        for c in range(width):
            summed = None
            for i, (j, n) in enumerate(window(c)):
                term = jnp.dot(p_buf[h, c, :, i * tile_len:(i + 1) * tile_len],
                               v_buf[j, n, :, head_cols(h)], preferred_element_type=jnp.float32)
                summed = term if summed is None else summed + term
            o_buf[c, :, head_cols(h)] = (summed * inv_buf[h, c]).astype(o_buf.dtype)
        for s in far_first:
            ox(h, s, me).start()
        local_out(h).start()
        return carry

    lax.fori_loop(0, local, mix, 0)

    for s in steps:
        kx(s, me).wait_send()
        qx(s, me).wait_send()
        for h in range(local):
            vx(h, s, me).wait_send()

    def sent(j):
        bz(j, opposite(j)).wait_send()
        for s in range(heads_axis):
            kz(j, s, opposite(j)).wait_send()
            for h in range(local):
                vz(j, h, s, opposite(j)).wait_send()

    each_neighbour(sent)
    for h in range(local):
        local_out(h).wait()
        for s in steps:
            ox(h, s, me).wait_send()
            ox(h, s, peer(s)).wait_recv()


def body(heads_axis, tok_axis, query, key, value, valid_rows):
    width, part, wide = query.shape
    rows_grid = tok_axis // TIME_TILES
    tile_len, feats = part * heads_axis, wide // heads_axis
    local = feats // HEAD_DIM
    slots = len(window_slots(rows_grid))
    row_index = jnp.arange(tile_len) // TILE_W % TILE_H
    bias = jnp.where(row_index[None, None, :] < valid_rows[:, None, None], 0.0, -jnp.inf)
    bias = jnp.broadcast_to(bias.astype(jnp.float32), (width, 8, tile_len))
    most = slots * min(width, 3) * tile_len
    dma = pltpu.SemaphoreType.DMA
    any_space = pl.BlockSpec(memory_space=pl.ANY)
    return pl.pallas_call(
        functools.partial(kernel, heads_axis, rows_grid),
        out_shape=jax.ShapeDtypeStruct(query.shape, query.dtype),
        in_specs=[any_space] * 4,
        out_specs=any_space,
        scratch_shapes=[
            pltpu.VMEM((width, tile_len, feats), jnp.bfloat16),
            pltpu.VMEM((slots, width, tile_len, feats), jnp.bfloat16),
            pltpu.VMEM((slots, width, tile_len, feats), jnp.bfloat16),
            pltpu.VMEM((slots, width, 8, tile_len), jnp.float32),
            pltpu.VMEM((3 if slots <= 3 else 1, tile_len, most), jnp.float32),
            pltpu.VMEM((local, width, tile_len, most), jnp.bfloat16),
            pltpu.VMEM((local, width, tile_len, HEAD_DIM), jnp.float32),
            pltpu.VMEM((width, tile_len, feats), jnp.bfloat16),
            dma((4 + local,)),
            dma((heads_axis,)), dma((heads_axis,)),
            dma((heads_axis,)), dma((heads_axis,)),
            dma((local, heads_axis)), dma((local, heads_axis)),
            dma((slots,)), dma((slots,)),
            dma((slots, heads_axis)), dma((slots, heads_axis)),
            dma((slots, local, heads_axis)), dma((slots, local, heads_axis)),
            dma((local, heads_axis)), dma((local, heads_axis)),
        ],
        compiler_params=pltpu.CompilerParams(
            collective_id=0, has_side_effects=True, vmem_limit_bytes=63_000_000
        ),
    )(query, key, value, bias)


def solution(mesh):
    placed = (
        P(("clips", "tok"), "head", None),
        P(("clips", "tok"), "head", None),
        P(("clips", "tok"), "head", None),
        P(("clips", "tok")),
    )
    return jax.shard_map(
        functools.partial(body, mesh.shape["head"], mesh.shape["tok"]),
        mesh=mesh,
        in_specs=placed,
        out_specs=P(("clips", "tok"), "head", None),
        check_vma=False,
    )
```

time: 206 us -> 41.6 us (0.20)
  local copies, waits for them, and re-layouts: 83.7 us -> 3.18 us
  Pallas kernels: 0 us -> 38.1 us
  matrix products: 30.1 us -> 0 us
  starting transfers between devices: 29.6 us -> 0 us
  loops' own time: 18.8 us -> 0 us
  waiting for transfers between devices: 16.2 us -> 0 us
  blocking collectives: 14.3 us -> 0 us
  other arithmetic: 11.1 us -> 0.07 us
    pallas_call x0 -> x1, Pallas kernels: none -> 38.1 us  [body(): pl.pallas_call(functools.partial(kernel, heads_axis, rows_grid), out_shap...]
    while x126 -> x0, local copies, waits for them, and re-layouts: 33.3 us -> none
    dot_general x18 -> x0, matrix products: 30.1 us -> none  [the longest x9 18.3 us: attend(): jnp.einsum('qd,kd->qk', queries, block_keys, preferred_element_type=jnp.f...]
    another operation x1 -> x0, loops' own time: 18.8 us -> none  [body(): results = lax.map(attend, jnp.arange(width * local, dtype=jnp.int32))]
    ppermute x6 -> x0, starting transfers between devices: 17.8 us -> none  [shifted(): return lax.ppermute(block, axis, route)]
    all_to_all x1 -> x0, blocking collectives: 14.3 us -> none  [body(): lax.all_to_all(attended, 'head', split_axis=1, concat_axis=2, tiled=True)]
    unnamed x16 -> x3, local copies, waits for them, and re-layouts: 15.9 us -> 2.57 us
    all_to_all x3 -> x0, starting transfers between devices: 11.9 us -> none  [the longest x1 4.24 us: body(): lax.all_to_all(key, 'head', split_axis=2, concat_axis=1, tiled=True)]
  transfers between devices with their start and end apart: 9 -> 0, of which waited for: 3 -> 0; matrix products, arithmetic and copies ran while one was open for 13% -> 0% of each run, Pallas kernels for 0% -> 0%
where the time goes in v1:
time: 41.6 us; the launch traced here: 41.4 us
  Pallas kernels  38.1 us (92%)
  local copies, waits for them, and re-layouts  3.18 us (8%)
    pallas_call x1, Pallas kernels, body(): pl.pallas_call(functools.partial(kernel, heads_axis, rows_grid), out_shap...  38.1 us
    unnamed x3, local copies, waits for them, and re-layouts  2.57 us

profile of v1, /device:TPU:0, one launch (start us, length us, event | category | flops | bytes accessed | tf_op | source)
XLA Modules:
  0.0 41.4 jit_solution(10735609264049003414)
XLA Ops:
  0.0 0.0 copy-start
  0.0 0.6 %copy-done = s32[3]{0:T(128)S(1)} copy-done((s32[3]{0:T(128)S(1)}, s32[3]{0:T(128)}, u32[]{:S(2)}) %copy-start) | copy-done | bytes 36
  0.7 0.1 compare_select_fusion
  0.7 0.6 %broadcast_in_dim.17.bias_hbm = f32[3,8,256]{2,1,0:T(8,128)} broadcast(f32[3,256]{1,0:T(4,128)S(1)} %compare_select_fusion), dimensions={0,2} | broadcast | bytes 27648 | tf_op jit(solution)/shard_map/broadcast_in_dim | solution.py:258
  1.3 38.1 %shard_map.46 = bf16[3,64,1536]{2,1,0:T(8,128)(2,1)} custom-call(bf16[3,64,1536]{2,1,0:T(8,128)(2,1)} %q_hbm.1, bf16[3,64,1536]{2,1,0:T(8,128)(2,1)} %k_hbm.1, bf16[3,64,1536]{2,1,0:T(8,128)(2,1)} %v_hbm.1, f32[3,8,256]{2,1,0:T(8,128)} %broadcast_in_dim.17.bias_hbm), custom_call_target="tpu_custom_call" | custom-call | tf_op jit(solution)/shard_map/pallas_call | solution.py:262
  39.5 1.9 %copy.6 = bf16[3,64,1536]{2,1,0:T(8,128)(2,1)} copy(bf16[3,64,1536]{2,1,0:T(8,128)(2,1)} %shard_map.46) | data formatting | bytes 1179648
  (1 shorter events, 0.0 us)
Async XLA Ops:
  0.0 0.7 %copy-start = (s32[3]{0:T(128)S(1)}, s32[3]{0:T(128)}, u32[]{:S(2)}) copy-start(s32[3]{0:T(128)} %param.7) | copy-start | bytes 40

commit v2 on v1

--- a/solution.py
+++ b/solution.py
@@ -24,8 +24,8 @@
 
 def kernel(
     heads_axis, rows_grid,
-    q_hbm, k_hbm, v_hbm, bias_hbm, out_hbm,
-    q_buf, k_buf, v_buf, bias_buf, s_buf, p_buf, inv_buf, o_buf,
+    q_hbm, k_hbm, v_hbm, count_hbm, out_hbm,
+    q_buf, k_buf, v_buf, bias_buf, s_buf, p_buf, inv_buf, acc_buf, o_buf, count_buf,
     local_sem, qx_send, qx_recv, kx_send, kx_recv, vx_send, vx_recv,
     bz_send, bz_recv, kz_send, kz_recv, vz_send, vz_recv, ox_send, ox_recv,
 ):
@@ -81,28 +81,28 @@
         return remote(k_hbm.at[:, :, cols(peer(s))], k_buf.at[0, :, rows(owner), :],
                       kx_send.at[s], kx_recv.at[s], {"head": peer(s)})
 
-    def vx(h, s, owner):
-        return remote(v_hbm.at[:, :, global_cols(peer(s), h)],
-                      v_buf.at[0, :, rows(owner), head_cols(h)],
-                      vx_send.at[h, s], vx_recv.at[h, s], {"head": peer(s)})
+    def vx(h, n, s, owner):
+        return remote(v_hbm.at[n, :, global_cols(peer(s), h)],
+                      v_buf.at[0, n, rows(owner), head_cols(h)],
+                      vx_send.at[h, n, s], vx_recv.at[h, n, s], {"head": peer(s)})
 
     def kz(j, s, slot):
         src = k_hbm.at[:, :, cols(me)] if s == 0 else k_buf.at[0, :, rows(peer(s)), :]
         return remote(src, k_buf.at[slot, :, rows(peer(s)), :],
                       kz_send.at[j, s], kz_recv.at[slot, s], {"tok": around(j)})
 
-    def vz(j, h, s, slot):
-        src = v_hbm.at[:, :, global_cols(me, h)] if s == 0 else v_buf.at[0, :, rows(peer(s)), head_cols(h)]
-        return remote(src, v_buf.at[slot, :, rows(peer(s)), head_cols(h)],
-                      vz_send.at[j, h, s], vz_recv.at[slot, h, s], {"tok": around(j)})
+    def vz(j, h, n, s, slot):
+        src = v_hbm.at[n, :, global_cols(me, h)] if s == 0 else v_buf.at[0, n, rows(peer(s)), head_cols(h)]
+        return remote(src, v_buf.at[slot, n, rows(peer(s)), head_cols(h)],
+                      vz_send.at[j, h, n, s], vz_recv.at[slot, h, n, s], {"tok": around(j)})
 
     def bz(j, slot):
-        return remote(bias_hbm, bias_buf.at[slot], bz_send.at[j], bz_recv.at[slot], {"tok": around(j)})
-
-    def ox(h, s, owner):
-        return remote(o_buf.at[:, rows(peer(s)), head_cols(h)],
-                      out_hbm.at[:, :, global_cols(owner, h)],
-                      ox_send.at[h, s], ox_recv.at[h, s], {"head": peer(s)})
+        return remote(bias_buf.at[0], bias_buf.at[slot], bz_send.at[j], bz_recv.at[slot], {"tok": around(j)})
+
+    def ox(h, c, s, owner):
+        return remote(o_buf.at[c, rows(peer(s)), head_cols(h)],
+                      out_hbm.at[c, :, global_cols(owner, h)],
+                      ox_send.at[h, c, s], ox_recv.at[h, c, s], {"head": peer(s)})
 
     def each_neighbour(act):
         for j in range(1, len(slots)):
@@ -111,7 +111,7 @@
     local_q = pltpu.make_async_copy(q_hbm.at[:, :, cols(me)], q_buf.at[:, rows(me), :], local_sem.at[0])
     local_k = pltpu.make_async_copy(k_hbm.at[:, :, cols(me)], k_buf.at[0, :, rows(me), :], local_sem.at[1])
     local_v = pltpu.make_async_copy(v_hbm.at[:, :, cols(me)], v_buf.at[0, :, rows(me), :], local_sem.at[2])
-    local_b = pltpu.make_async_copy(bias_hbm, bias_buf.at[0], local_sem.at[3])
+    local_c = pltpu.make_async_copy(count_hbm, count_buf, local_sem.at[3])
 
     barrier = pltpu.get_barrier_semaphore()
     for s in steps:
@@ -124,19 +124,24 @@
     each_neighbour(greet)
     for j in range(1, len(slots)):
         partners = partners + jnp.where(exists(j), 1, 0)
-    for copy in (local_q, local_k, local_v, local_b):
+    for copy in (local_c, local_q, local_k, local_v):
         copy.start()
     pl.semaphore_wait(barrier, partners)
 
-    each_neighbour(lambda j: bz(j, opposite(j)).start())
     for s in far_first:
         kx(s, me).start()
     each_neighbour(lambda j: kz(j, 0, opposite(j)).start())
     for s in far_first:
         qx(s, me).start()
     for h in range(local):
-        for s in far_first:
-            vx(h, s, me).start()
+        for n in range(width):
+            for s in far_first:
+                vx(h, n, s, me).start()
+
+    local_c.wait()
+    row = lax.broadcasted_iota(jnp.int32, bias_buf.shape[2:], 1) // TILE_W % TILE_H
+    for n in range(width):
+        bias_buf[0, n] = jnp.where(row < count_buf[n], 0.0, -jnp.inf)
 
     for j in range(1, len(slots)):
         @pl.when(jnp.logical_not(exists(j)))
@@ -151,13 +156,19 @@
         each_neighbour(lambda j, s=s: kz(j, s, opposite(j)).start())
     near = [s for s in steps if s == 1]
     later = [s for s in order if s != 1]
+    each_neighbour(lambda j: bz(j, opposite(j)).start())
+
+    def values_on(h, n, s):
+        if s != 0:
+            vx(h, n, s, peer(s)).wait_recv()
+        each_neighbour(lambda j: vz(j, h, n, s, opposite(j)).start())
+
     for h in range(local):
-        each_neighbour(lambda j, h=h: vz(j, h, 0, opposite(j)).start())
-        for s in near:
-            vx(h, s, peer(s)).wait_recv()
-            each_neighbour(lambda j, h=h, s=s: vz(j, h, s, opposite(j)).start())
-
-    for copy in (local_q, local_k, local_v, local_b):
+        for n in range(width):
+            for s in [0] + near:
+                values_on(h, n, s)
+
+    for copy in (local_q, local_k, local_v):
         copy.wait()
     for s in steps:
         qx(s, peer(s)).wait_recv()
@@ -195,33 +206,49 @@
                     p_buf[h, c, :, at] = weight.astype(jnp.bfloat16)
             inverse = 1.0 / jnp.sum(total, axis=-1, keepdims=True)
             inv_buf[h, c] = jnp.broadcast_to(inverse, (tile_len, HEAD_DIM))
-        for s in later:
-            vx(h, s, peer(s)).wait_recv()
-            each_neighbour(lambda j, s=s: vz(j, h, s, opposite(j)).start())
+        for n in range(width):
+            for s in later:
+                values_on(h, n, s)
         return carry
 
     lax.fori_loop(0, local, weigh, 0)
 
-    def local_out(h):
-        return pltpu.make_async_copy(o_buf.at[:, rows(me), head_cols(h)],
-                                     out_hbm.at[:, :, global_cols(me, h)], local_sem.at[4 + h])
+    def local_out(h, c):
+        return pltpu.make_async_copy(o_buf.at[c, rows(me), head_cols(h)],
+                                     out_hbm.at[c, :, global_cols(me, h)], local_sem.at[4 + h * width + c])
 
     def mix(h, carry):
-        def values_in(j):
-            for s in range(heads_axis):
-                vz(j, h, s, j).wait_recv()
-
-        each_neighbour(values_in)
-        for c in range(width):
+        def gather(c, picked):
             summed = None
             for i, (j, n) in enumerate(window(c)):
-                term = jnp.dot(p_buf[h, c, :, i * tile_len:(i + 1) * tile_len],
-                               v_buf[j, n, :, head_cols(h)], preferred_element_type=jnp.float32)
-                summed = term if summed is None else summed + term
-            o_buf[c, :, head_cols(h)] = (summed * inv_buf[h, c]).astype(o_buf.dtype)
-        for s in far_first:
-            ox(h, s, me).start()
-        local_out(h).start()
+                if picked(j, n):
+                    term = jnp.dot(p_buf[h, c, :, i * tile_len:(i + 1) * tile_len],
+                                   v_buf[j, n, :, head_cols(h)], preferred_element_type=jnp.float32)
+                    summed = term if summed is None else summed + term
+            return summed
+
+        for c in range(width):
+            acc_buf[c] = gather(c, lambda j, n: j == 0)
+        for n in range(width):
+            def values_in(j, n=n):
+                for s in range(heads_axis):
+                    vz(j, h, n, s, j).wait_recv()
+
+            each_neighbour(values_in)
+            done = []
+            for c in range(width):
+                if abs(n - c) <= 1:
+                    summed = acc_buf[c] + gather(c, lambda j, m: j != 0 and m == n)
+                    if n == min(c + 1, width - 1):
+                        o_buf[c, :, head_cols(h)] = (summed * inv_buf[h, c]).astype(o_buf.dtype)
+                        done.append(c)
+                    else:
+                        acc_buf[c] = summed
+            for s in far_first:
+                for c in done:
+                    ox(h, c, s, me).start()
+            for c in done:
+                local_out(h, c).start()
         return carry
 
     lax.fori_loop(0, local, mix, 0)
@@ -230,21 +257,24 @@
         kx(s, me).wait_send()
         qx(s, me).wait_send()
         for h in range(local):
-            vx(h, s, me).wait_send()
+            for n in range(width):
+                vx(h, n, s, me).wait_send()
 
     def sent(j):
         bz(j, opposite(j)).wait_send()
         for s in range(heads_axis):
             kz(j, s, opposite(j)).wait_send()
             for h in range(local):
-                vz(j, h, s, opposite(j)).wait_send()
+                for n in range(width):
+                    vz(j, h, n, s, opposite(j)).wait_send()
 
     each_neighbour(sent)
     for h in range(local):
-        local_out(h).wait()
-        for s in steps:
-            ox(h, s, me).wait_send()
-            ox(h, s, peer(s)).wait_recv()
+        for c in range(width):
+            local_out(h, c).wait()
+            for s in steps:
+                ox(h, c, s, me).wait_send()
+                ox(h, c, s, peer(s)).wait_recv()
 
 
 def body(heads_axis, tok_axis, query, key, value, valid_rows):
@@ -253,16 +283,13 @@
     tile_len, feats = part * heads_axis, wide // heads_axis
     local = feats // HEAD_DIM
     slots = len(window_slots(rows_grid))
-    row_index = jnp.arange(tile_len) // TILE_W % TILE_H
-    bias = jnp.where(row_index[None, None, :] < valid_rows[:, None, None], 0.0, -jnp.inf)
-    bias = jnp.broadcast_to(bias.astype(jnp.float32), (width, 8, tile_len))
     most = slots * min(width, 3) * tile_len
     dma = pltpu.SemaphoreType.DMA
     any_space = pl.BlockSpec(memory_space=pl.ANY)
     return pl.pallas_call(
         functools.partial(kernel, heads_axis, rows_grid),
         out_shape=jax.ShapeDtypeStruct(query.shape, query.dtype),
-        in_specs=[any_space] * 4,
+        in_specs=[pl.BlockSpec(memory_space=pltpu.HBM)] * 4,
         out_specs=any_space,
         scratch_shapes=[
             pltpu.VMEM((width, tile_len, feats), jnp.bfloat16),
@@ -272,20 +299,22 @@
             pltpu.VMEM((3 if slots <= 3 else 1, tile_len, most), jnp.float32),
             pltpu.VMEM((local, width, tile_len, most), jnp.bfloat16),
             pltpu.VMEM((local, width, tile_len, HEAD_DIM), jnp.float32),
+            pltpu.VMEM((width, tile_len, HEAD_DIM), jnp.float32),
             pltpu.VMEM((width, tile_len, feats), jnp.bfloat16),
-            dma((4 + local,)),
+            pltpu.SMEM((width,), jnp.int32),
+            dma((4 + local * width,)),
             dma((heads_axis,)), dma((heads_axis,)),
             dma((heads_axis,)), dma((heads_axis,)),
-            dma((local, heads_axis)), dma((local, heads_axis)),
+            dma((local, width, heads_axis)), dma((local, width, heads_axis)),
             dma((slots,)), dma((slots,)),
             dma((slots, heads_axis)), dma((slots, heads_axis)),
-            dma((slots, local, heads_axis)), dma((slots, local, heads_axis)),
-            dma((local, heads_axis)), dma((local, heads_axis)),
+            dma((slots, local, width, heads_axis)), dma((slots, local, width, heads_axis)),
+            dma((local, width, heads_axis)), dma((local, width, heads_axis)),
         ],
         compiler_params=pltpu.CompilerParams(
-            collective_id=0, has_side_effects=True, vmem_limit_bytes=63_000_000
+            collective_id=0, has_side_effects=True, vmem_limit_bytes=36_000_000 if slots <= 3 else 63_000_000
         ),
-    )(query, key, value, bias)
+    )(*(pltpu.with_memory_space_constraint(x, pltpu.HBM) for x in (query, key, value, valid_rows)))
 
 
 def solution(mesh):

time: 41.6 us -> 40.2 us (0.966)
  local copies, waits for them, and re-layouts: 3.18 us -> 0.82 us
  Pallas kernels: 38.1 us -> 39.2 us
    unnamed x3 -> x1, local copies, waits for them, and re-layouts: 2.57 us -> 0.82 us
    pallas_call x1, Pallas kernels: 38.1 us -> 39.2 us  [body(): pl.pallas_call(functools.partial(kernel, heads_axis, rows_grid), out_shap...]
    broadcast_in_dim x1 -> x0, local copies, waits for them, and re-layouts: 0.61 us -> none  [body(): bias = jnp.broadcast_to(bias.astype(jnp.float32), (width, 8, tile_len))]
where the time goes in v2:
time: 40.2 us; the launch traced here: 40 us
  Pallas kernels  39.2 us (98%)
  local copies, waits for them, and re-layouts  0.82 us (2%)
    pallas_call x1, Pallas kernels, body(): pl.pallas_call(functools.partial(kernel, heads_axis, rows_grid), out_shap...  39.2 us
    unnamed x1, local copies, waits for them, and re-layouts  0.82 us

profile of v2, /device:TPU:0, one launch (start us, length us, event | category | flops | bytes accessed | tf_op | source)
XLA Modules:
  0.0 40.0 jit_solution(971888298667664755)
XLA Ops:
  0.0 39.2 %shard_map.46 = bf16[3,64,1536]{2,1,0:T(8,128)(2,1)S(1)} custom-call(bf16[3,64,1536]{2,1,0:T(8,128)(2,1)} %q_hbm.1, bf16[3,64,1536]{2,1,0:T(8,128)(2,1)} %k_hbm.1, bf16[3,64,1536]{2,1,0:T(8,128)(2,1)} %v_hbm.1, s32[3]{0:T(128)} %count_hbm.1), custom_call_target="tpu_custom_call" | custom-call | tf_op jit(solution)/shard_map/pallas_call | solution.py:289
  39.2 0.8 %copy.6 = bf16[3,64,1536]{2,1,0:T(8,128)(2,1)} copy(bf16[3,64,1536]{2,1,0:T(8,128)(2,1)S(1)} %shard_map.46) | data formatting | bytes 1179648

commit v3 on v2

--- a/solution.py
+++ b/solution.py
@@ -25,7 +25,7 @@
 def kernel(
     heads_axis, rows_grid,
     q_hbm, k_hbm, v_hbm, count_hbm, out_hbm,
-    q_buf, k_buf, v_buf, bias_buf, s_buf, p_buf, inv_buf, acc_buf, o_buf, count_buf,
+    q_buf, k_buf, v_buf, bias_buf, s_buf, p_buf, inv_buf, acc_buf, o_buf, rows_buf, count_buf,
     local_sem, qx_send, qx_recv, kx_send, kx_recv, vx_send, vx_recv,
     bz_send, bz_recv, kz_send, kz_recv, vz_send, vz_recv, ox_send, ox_recv,
 ):
@@ -97,7 +97,7 @@
                       vz_send.at[j, h, n, s], vz_recv.at[slot, h, n, s], {"tok": around(j)})
 
     def bz(j, slot):
-        return remote(bias_buf.at[0], bias_buf.at[slot], bz_send.at[j], bz_recv.at[slot], {"tok": around(j)})
+        return remote(rows_buf.at[0], rows_buf.at[slot], bz_send.at[j], bz_recv.at[slot], {"tok": around(j)})
 
     def ox(h, c, s, owner):
         return remote(o_buf.at[c, rows(peer(s)), head_cols(h)],
@@ -139,16 +139,18 @@
                 vx(h, n, s, me).start()
 
     local_c.wait()
-    row = lax.broadcasted_iota(jnp.int32, bias_buf.shape[2:], 1) // TILE_W % TILE_H
+    line = lax.broadcasted_iota(jnp.int32, rows_buf.shape[1:], 0)
+    counts = jnp.zeros(rows_buf.shape[1:], jnp.int32)
     for n in range(width):
-        bias_buf[0, n] = jnp.where(row < count_buf[n], 0.0, -jnp.inf)
+        counts = jnp.where(line == n, count_buf[n], counts)
+    rows_buf[0] = counts
 
     for j in range(1, len(slots)):
         @pl.when(jnp.logical_not(exists(j)))
         def _(j=j):
             k_buf[j] = jnp.zeros(k_buf.shape[1:], k_buf.dtype)
             v_buf[j] = jnp.zeros(v_buf.shape[1:], v_buf.dtype)
-            bias_buf[j] = jnp.full(bias_buf.shape[1:], -jnp.inf, bias_buf.dtype)
+            rows_buf[j] = jnp.zeros(rows_buf.shape[1:], rows_buf.dtype)
 
     order = [1] + [s for s in far_first if s != 1] if heads_axis > 1 else []
     for s in order:
@@ -179,6 +181,12 @@
             kz(j, s, j).wait_recv()
 
     each_neighbour(keys_in)
+
+    row = lax.broadcasted_iota(jnp.int32, bias_buf.shape[2:], 1) // TILE_W % TILE_H
+    for j in range(len(slots)):
+        for n in range(width):
+            real = jnp.broadcast_to(rows_buf[j, n:n + 1, 0:1], row.shape)
+            bias_buf[j, n] = jnp.where(row < real, 0.0, -jnp.inf)
 
     def window(c):
         return [(j, n) for j in range(len(slots)) for n in range(width) if abs(n - c) <= 1]
@@ -217,38 +225,48 @@
         return pltpu.make_async_copy(o_buf.at[c, rows(me), head_cols(h)],
                                      out_hbm.at[c, :, global_cols(me, h)], local_sem.at[4 + h * width + c])
 
+    if heads_axis % 2 == 0:
+        half = heads_axis // 2
+        span = tile_len // 2
+        side = me // half
+        blocks = [
+            (pl.ds(pl.multiple_of((1 - side) * span, span), span), [s for s in far_first if s >= half]),
+            (pl.ds(pl.multiple_of(side * span, span), span), [s for s in far_first if s < half]),
+        ]
+    else:
+        blocks = [(slice(None), far_first)]
+
     def mix(h, carry):
-        def gather(c, picked):
+        def gather(c, at, picked):
             summed = None
             for i, (j, n) in enumerate(window(c)):
                 if picked(j, n):
-                    term = jnp.dot(p_buf[h, c, :, i * tile_len:(i + 1) * tile_len],
+                    term = jnp.dot(p_buf[h, c, at, i * tile_len:(i + 1) * tile_len],
                                    v_buf[j, n, :, head_cols(h)], preferred_element_type=jnp.float32)
                     summed = term if summed is None else summed + term
             return summed
 
         for c in range(width):
-            acc_buf[c] = gather(c, lambda j, n: j == 0)
+            acc_buf[c] = gather(c, slice(None), lambda j, n: j == 0)
         for n in range(width):
             def values_in(j, n=n):
                 for s in range(heads_axis):
                     vz(j, h, n, s, j).wait_recv()
 
             each_neighbour(values_in)
-            done = []
-            for c in range(width):
-                if abs(n - c) <= 1:
-                    summed = acc_buf[c] + gather(c, lambda j, m: j != 0 and m == n)
-                    if n == min(c + 1, width - 1):
-                        o_buf[c, :, head_cols(h)] = (summed * inv_buf[h, c]).astype(o_buf.dtype)
-                        done.append(c)
-                    else:
-                        acc_buf[c] = summed
-            for s in far_first:
+            here = [c for c in range(width) if abs(n - c) <= 1]
+            done = [c for c in here if n == min(c + 1, width - 1)]
+            for at, partners_at in blocks:
                 for c in done:
-                    ox(h, c, s, me).start()
+                    summed = acc_buf[c, at] + gather(c, at, lambda j, m: j != 0 and m == n)
+                    o_buf[c, at, head_cols(h)] = (summed * inv_buf[h, c, at]).astype(o_buf.dtype)
+                    for s in partners_at:
+                        ox(h, c, s, me).start()
             for c in done:
                 local_out(h, c).start()
+            for c in here:
+                if c not in done:
+                    acc_buf[c] = acc_buf[c] + gather(c, slice(None), lambda j, m: j != 0 and m == n)
         return carry
 
     lax.fori_loop(0, local, mix, 0)
@@ -301,6 +319,7 @@
             pltpu.VMEM((local, width, tile_len, HEAD_DIM), jnp.float32),
             pltpu.VMEM((width, tile_len, HEAD_DIM), jnp.float32),
             pltpu.VMEM((width, tile_len, feats), jnp.bfloat16),
+            pltpu.VMEM((slots, -(-width // 8) * 8, 128), jnp.int32),
             pltpu.SMEM((width,), jnp.int32),
             dma((4 + local * width,)),
             dma((heads_axis,)), dma((heads_axis,)),

time: 40.2 us -> 39.8 us (0.990)
  no operation moved by 1% of the time
where the time goes in v3:
time: 39.8 us; the launch traced here: 39.7 us
  Pallas kernels  38.9 us (98%)
  local copies, waits for them, and re-layouts  0.82 us (2%)
    pallas_call x1, Pallas kernels, body(): pl.pallas_call(functools.partial(kernel, heads_axis, rows_grid), out_shap...  38.9 us
    unnamed x1, local copies, waits for them, and re-layouts  0.82 us

profile of v3, /device:TPU:0, one launch (start us, length us, event | category | flops | bytes accessed | tf_op | source)
XLA Modules:
  0.0 39.7 jit_solution(15981096140792327244)
XLA Ops:
  0.0 38.9 %shard_map.46 = bf16[3,64,1536]{2,1,0:T(8,128)(2,1)S(1)} custom-call(bf16[3,64,1536]{2,1,0:T(8,128)(2,1)} %q_hbm.1, bf16[3,64,1536]{2,1,0:T(8,128)(2,1)} %k_hbm.1, bf16[3,64,1536]{2,1,0:T(8,128)(2,1)} %v_hbm.1, s32[3]{0:T(128)} %count_hbm.1), custom_call_target="tpu_custom_call" | custom-call | tf_op jit(solution)/shard_map/pallas_call | solution.py:307
  38.9 0.8 %copy.6 = bf16[3,64,1536]{2,1,0:T(8,128)(2,1)} copy(bf16[3,64,1536]{2,1,0:T(8,128)(2,1)S(1)} %shard_map.46) | data formatting | bytes 1179648
